TPU v7x, 32 devices: a whole 2x2x4 slice. The times are simulated.
32 devices in a mesh: fsdp: 8 (over y, x, core), seq: 4 (over z).
Axes of the slice: x: 2, y: 2, z: 4, core: 2. Of those that a mesh axis runs over, the one named last changes fastest.
Arguments:
- latents_in: bfloat16 [2, 8, 128, 768], P(None, 'fsdp'), may hold values from -6 to 6
- inputs: bfloat16 [2, 8, 6312, 768], P(None, 'fsdp', 'seq'), may hold values from -6 to 6
- clip_frames: int32 [2, 8], P(None, 'fsdp'), may hold values from 4 to 16
- text_mask: int32 [2, 8, 40], P(None, 'fsdp'), may hold values 0 or 1
- qkv_weight: bfloat16 [2, 3, 768, 768], P(None, None, 'fsdp'), may hold values from -0.21875 to 0.21875
- out_weight: bfloat16 [2, 768, 768], P(None, 'fsdp'), may hold values from -1.75 to 1.75
- mlp_in: bfloat16 [2, 768, 3072], P(None, 'fsdp'), may hold values from -0.21875 to 0.21875
- mlp_out: bfloat16 [2, 3072, 768], P(None, 'fsdp'), may hold values from -0.109375 to 0.109375
- norm_gain: bfloat16 [5, 768], P(None, 'fsdp'), may hold values from 0.5 to 1.5
- norm_bias: bfloat16 [5, 768], P(None, 'fsdp'), may hold values from -2.5 to 2.5
- bias_in: bfloat16 [2, 3072], P(None, 'fsdp'), may hold values from -2.5 to 2.5
- bias_out: bfloat16 [2, 768], P(None, 'fsdp'), may hold values from -2.5 to 2.5
- out_cotangent: bfloat16 [2, 8, 128, 768], P(None, 'fsdp'), may hold values from -6 to 6
Outputs:
- latents_out: float32 [2, 8, 128, 768], P(None, 'fsdp')
- latents_grad: float32 [2, 8, 128, 768], P(None, 'fsdp')
- inputs_grad: float32 [2, 8, 6312, 768], P(None, 'fsdp', 'seq')
- qkv_grad: float32 [2, 3, 768, 768], P(None, None, 'fsdp')
- out_weight_grad: float32 [2, 768, 768], P(None, 'fsdp')
- mlp_in_grad: float32 [2, 768, 3072], P(None, 'fsdp')
- mlp_out_grad: float32 [2, 3072, 768], P(None, 'fsdp')
- norm_gain_grad: float32 [5, 768], P(None, 'fsdp')
- norm_bias_grad: float32 [5, 768], P(None, 'fsdp')
- bias_in_grad: float32 [2, 3072], P(None, 'fsdp')
- bias_out_grad: float32 [2, 768], P(None, 'fsdp')
Inputs may be any that keep to these rules, and one draw needn't show every extreme that they name: `clip_frames`: frames of each clip; its first 392 times that many patch slots hold tokens, the rest of its 16 frame slots are padding.
All inputs are finite; a program needn't handle non-finite values. No bound on the sum of `text_mask` on one device may be relied on, other than what follows from the above.
Results may differ from a plain program's by a relative error of at most 0.015.
Values may be sent and summed in bfloat16 or wider, within the bound.
No kernel may reach another device: no remote copies, remote signals or barrier semaphores. Data moves between devices by JAX's collectives and lax.ppermute only.
A program may use at most 320 MiB of HBM per device.

v0:
```python
import jax
import jax.numpy as jnp
from jax import lax
from jax.sharding import PartitionSpec as P

D = 768
HEADS = 12
HEAD = 64
PATCHES = 392
FRAMES = 16
epsilon = 1e-06


def layer_norm(values, scales, offsets):
    center = values - jnp.mean(values, -1, keepdims=True)
    spread = jnp.mean(center * center, -1, keepdims=True)
    return center * lax.rsqrt(spread + epsilon) * scales + offsets


def to_half(values):
    return values.astype(jnp.bfloat16)


def product(form, left, right):
    return jnp.einsum(form, left, right, preferred_element_type=jnp.float32)


def norm_back(values, scales, offsets, grad_normed):
    unused, pullback = jax.vjp(layer_norm, values, scales, offsets)
    return pullback(grad_normed)


def feed_forward(residual, up_w, down_w, up_b, down_b, scales, offsets):
    normed = to_half(layer_norm(residual, scales, offsets))
    hidden = product("cnd,df->cnf", normed, up_w) + up_b
    active = to_half(jax.nn.gelu(hidden))
    result = product("cnf,fd->cnd", active, down_w) + down_b
    return (result, (residual, normed, hidden, active))


def feed_back(stored, grad_in, up_w, down_w, scales, offsets):
    residual, normed, hidden, active = stored
    grad_y = to_half(grad_in)
    grad_down = product("cnf,cnd->fd", active, grad_y)
    grad_down_b = jnp.sum(grad_y, (0, 1), dtype=jnp.float32)
    grad_act = product("cnd,fd->cnf", grad_y, down_w)
    unused, gelu_pull = jax.vjp(jax.nn.gelu, hidden)
    grad_hidden = to_half(gelu_pull(grad_act)[0])
    grad_up = product("cnd,cnf->df", normed, grad_hidden)
    grad_up_b = jnp.sum(grad_hidden, (0, 1), dtype=jnp.float32)
    grad_normed = product("cnf,df->cnd", grad_hidden, up_w)
    grad_rows, grad_scales, grad_offsets = norm_back(residual, scales, offsets, grad_normed)
    return (grad_rows, (grad_up, grad_down, grad_up_b, grad_down_b, grad_scales, grad_offsets))


def self_forward(residual, qkv_w, out_w, scales, offsets):
    clip_count, latent_count = (residual.shape[0], residual.shape[1])
    normed = to_half(layer_norm(residual, scales, offsets))
    heads_qkv = to_half(product("cnd,jde->jcne", normed, qkv_w)).reshape(
        3, clip_count, latent_count, HEADS, HEAD
    )
    scores = product("cqhd,ckhd->cqhk", heads_qkv[0], heads_qkv[1]) * 0.125
    row_peak = jnp.max(scores, -1, keepdims=True)
    self_exp = jnp.exp(scores - row_peak)
    softmax_w = self_exp / jnp.sum(self_exp, -1, keepdims=True)
    mixed_heads = to_half(product("cqhk,ckhd->cqhd", to_half(softmax_w), heads_qkv[2])).reshape(
        clip_count, latent_count, D
    )
    result = product("cnd,de->cne", mixed_heads, out_w)
    return (result, (residual, normed, heads_qkv, softmax_w, mixed_heads))


def self_back(stored, grad_in, qkv_w, out_w, scales, offsets):
    residual, normed, heads_qkv, softmax_w, mixed_heads = stored
    clip_count, latent_count = (residual.shape[0], residual.shape[1])
    grad_a = to_half(grad_in)
    grad_out_w = product("cnd,cne->de", mixed_heads, grad_a)
    grad_mixed = to_half(product("cne,de->cnd", grad_a, out_w)).reshape(
        clip_count, latent_count, HEADS, HEAD
    )
    grad_probs = product("cqhd,ckhd->cqhk", grad_mixed, heads_qkv[2])
    grad_values = to_half(product("cqhk,cqhd->ckhd", to_half(softmax_w), grad_mixed))
    grad_scores = to_half(
        softmax_w * (grad_probs - jnp.sum(softmax_w * grad_probs, -1, keepdims=True))
    )
    grad_queries = to_half(product("cqhk,ckhd->cqhd", grad_scores, heads_qkv[1]) * 0.125)
    grad_keys = to_half(product("cqhk,cqhd->ckhd", grad_scores, heads_qkv[0]) * 0.125)
    stacked = jnp.stack([grad_queries, grad_keys, grad_values]).reshape(
        3, clip_count, latent_count, D
    )
    grad_qkv = product("cnd,jcne->jde", normed, stacked)
    grad_normed = product("jcne,jde->cnd", stacked, qkv_w)
    grad_rows, grad_scales, grad_offsets = norm_back(residual, scales, offsets, grad_normed)
    return (grad_rows, (grad_qkv, grad_out_w, grad_scales, grad_offsets))


def cross_scores(queries, key_heads, valid_keys):
    scores = product("cqhd,ckhd->cqhk", queries, key_heads) * 0.125
    return jnp.where(valid_keys[:, None, None, :], jnp.exp(scores), 0.0)


def cross_forward(residual, tokens, valid_keys, qkv_w, out_w, scales, offsets):
    clip_count, latent_count, local_len = (residual.shape[0], residual.shape[1], tokens.shape[1])
    latent_normed = to_half(layer_norm(residual, scales[0], offsets[0]))
    token_normed = to_half(layer_norm(tokens, scales[1], offsets[1]))
    queries = to_half(product("cnd,de->cne", latent_normed, qkv_w[0])).reshape(
        clip_count, latent_count, HEADS, HEAD
    )
    keyval = to_half(product("cld,jde->jcle", token_normed, qkv_w[1:3])).reshape(
        2, clip_count, local_len, HEADS, HEAD
    )
    weights_exp = cross_scores(queries, keyval[0], valid_keys)
    numer_part = product("cqhk,ckhd->cqhd", to_half(weights_exp), keyval[1])
    numer_share, total_share = (
        lax.psum_scatter(numer_part, "seq", scatter_dimension=2, tiled=True),
        lax.psum_scatter(jnp.sum(weights_exp, -1), "seq", scatter_dimension=2, tiled=True),
    )
    numerator, totals = (
        lax.all_gather(numer_share, "seq", axis=2, tiled=True),
        lax.all_gather(total_share, "seq", axis=2, tiled=True),
    )
    attended = to_half(numerator / totals[..., None]).reshape(clip_count, latent_count, D)
    result = product("cnd,de->cne", attended, out_w)
    return (
        result,
        (
            residual,
            tokens,
            latent_normed,
            token_normed,
            queries,
            keyval,
            numerator,
            totals,
            attended,
        ),
    )


def cross_back(stored, grad_in, valid_keys, qkv_w, out_w, scales, offsets):
    residual, tokens, latent_normed, token_normed, queries, keyval, numerator, totals, attended = (
        stored
    )
    clip_count, latent_count, local_len = (residual.shape[0], residual.shape[1], tokens.shape[1])
    grad_a = to_half(grad_in)
    grad_out_w = product("cnd,cne->de", attended, grad_a)
    grad_att = (
        to_half(product("cne,de->cnd", grad_a, out_w))
        .reshape(clip_count, latent_count, HEADS, HEAD)
        .astype(jnp.float32)
    )
    grad_numer = to_half(grad_att / totals[..., None])
    grad_totals = -jnp.sum(grad_att * numerator, -1) / (totals * totals)
    weights_exp = cross_scores(queries, keyval[0], valid_keys)
    grad_weights = product("cqhd,ckhd->cqhk", grad_numer, keyval[1]) + grad_totals[..., None]
    grad_scores = to_half(weights_exp * grad_weights)
    grad_values = to_half(product("cqhk,cqhd->ckhd", to_half(weights_exp), grad_numer))
    grad_keys = to_half(product("cqhk,cqhd->ckhd", grad_scores, queries) * 0.125)
    grad_query_part = product("cqhk,ckhd->cqhd", grad_scores, keyval[0]) * 0.125
    query_share = lax.psum_scatter(
        grad_query_part.astype(jnp.bfloat16), "seq", scatter_dimension=2, tiled=True
    ).astype(jnp.float32)
    grad_queries = lax.all_gather(to_half(query_share), "seq", axis=2, tiled=True).reshape(
        clip_count, latent_count, D
    )
    grad_kv = jnp.stack([grad_keys, grad_values]).reshape(2, clip_count, local_len, D)
    grad_q_w = product("cnd,cne->de", latent_normed, grad_queries)
    grad_kv_w = product("cld,jcle->jde", token_normed, grad_kv)
    grad_latent_norm = product("cne,de->cnd", grad_queries, qkv_w[0])
    grad_token_norm = product("jcle,jde->cld", grad_kv, qkv_w[1:3])
    grad_rows, grad_scale_lat, grad_shift_lat = norm_back(
        residual, scales[0], offsets[0], grad_latent_norm
    )
    grad_tokens, grad_scale_tok, grad_shift_tok = norm_back(
        tokens, scales[1], offsets[1], grad_token_norm
    )
    grad_qkv = jnp.concatenate([grad_q_w[None], grad_kv_w])
    return (
        grad_rows,
        grad_tokens,
        (
            grad_qkv,
            grad_out_w,
            jnp.stack([grad_scale_lat, grad_scale_tok]),
            jnp.stack([grad_shift_lat, grad_shift_tok]),
        ),
    )


def per_device(
    latents_in,
    inputs,
    clip_frames,
    text_mask,
    qkv_weight,
    out_weight,
    mlp_in,
    mlp_out,
    norm_gain,
    norm_bias,
    bias_in,
    bias_out,
    out_cotangent,
):
    local_len = inputs.shape[2]
    seq_start = lax.axis_index("seq") * local_len
    positions = jnp.arange(FRAMES * PATCHES, dtype=jnp.int32)
    grad_sum = None
    finals = []
    latent_grads = []
    token_grads = []
    for micro_step in range(latents_in.shape[0]):
        gathered = (
            lax.all_gather(qkv_weight, "fsdp", axis=2, tiled=True),
            lax.all_gather(out_weight, "fsdp", axis=1, tiled=True),
            lax.all_gather(mlp_in, "fsdp", axis=1, tiled=True),
            lax.all_gather(mlp_out, "fsdp", axis=1, tiled=True),
            lax.all_gather(norm_gain, "fsdp", axis=1, tiled=True),
            lax.all_gather(norm_bias, "fsdp", axis=1, tiled=True),
            lax.all_gather(bias_in, "fsdp", axis=1, tiled=True),
            lax.all_gather(bias_out, "fsdp", axis=1, tiled=True),
        )
        qkv_w, out_w, up_w, down_w, gain_w, shift_w, up_bias, down_bias = gathered
        scales = gain_w.astype(jnp.float32)
        offsets = shift_w.astype(jnp.float32)
        up_b32 = up_bias.astype(jnp.float32)
        down_b32 = down_bias.astype(jnp.float32)
        frames_now = clip_frames[micro_step]
        full_mask = jnp.concatenate(
            [positions[None, :] < frames_now[:, None] * PATCHES, text_mask[micro_step] > 0], axis=1
        )
        valid_keys = lax.dynamic_slice_in_dim(full_mask, seq_start, local_len, 1)
        start_rows = latents_in[micro_step].astype(jnp.float32)
        token_rows = inputs[micro_step].astype(jnp.float32)
        cross_out, cross_saved = cross_forward(
            start_rows, token_rows, valid_keys, qkv_w[0], out_w[0], scales, offsets
        )
        first = start_rows + cross_out
        ff_one, ff_one_saved = feed_forward(
            first, up_w[0], down_w[0], up_b32[0], down_b32[0], scales[2], offsets[2]
        )
        second = first + ff_one
        self_out, self_saved = self_forward(second, qkv_w[1], out_w[1], scales[3], offsets[3])
        third = second + self_out
        ff_two, ff_two_saved = feed_forward(
            third, up_w[1], down_w[1], up_b32[1], down_b32[1], scales[4], offsets[4]
        )
        finals.append(third + ff_two)
        gathered = (
            lax.all_gather(qkv_weight, "fsdp", axis=2, tiled=True),
            lax.all_gather(out_weight, "fsdp", axis=1, tiled=True),
            lax.all_gather(mlp_in, "fsdp", axis=1, tiled=True),
            lax.all_gather(mlp_out, "fsdp", axis=1, tiled=True),
            lax.all_gather(norm_gain, "fsdp", axis=1, tiled=True),
            lax.all_gather(norm_bias, "fsdp", axis=1, tiled=True),
            lax.all_gather(bias_in, "fsdp", axis=1, tiled=True),
            lax.all_gather(bias_out, "fsdp", axis=1, tiled=True),
        )
        qkv_w, out_w, up_w, down_w, gain_w, shift_w, up_bias, down_bias = gathered
        scales = gain_w.astype(jnp.float32)
        offsets = shift_w.astype(jnp.float32)
        grad_four = out_cotangent[micro_step].astype(jnp.float32)
        grad_three, ff_two_grads = feed_back(
            ff_two_saved, grad_four, up_w[1], down_w[1], scales[4], offsets[4]
        )
        grad_three = grad_three + grad_four
        grad_two, self_grads = self_back(
            self_saved, grad_three, qkv_w[1], out_w[1], scales[3], offsets[3]
        )
        grad_two = grad_two + grad_three
        grad_one, ff_one_grads = feed_back(
            ff_one_saved, grad_two, up_w[0], down_w[0], scales[2], offsets[2]
        )
        grad_one = grad_one + grad_two
        grad_start, grad_tokens, cross_grads = cross_back(
            cross_saved, grad_one, valid_keys, qkv_w[0], out_w[0], scales, offsets
        )
        latent_grads.append(grad_start + grad_one)
        token_grads.append(grad_tokens)
        grad_qkv_all = jnp.stack([cross_grads[0], self_grads[0]])
        grad_out_all = jnp.stack([cross_grads[1], self_grads[1]])
        grad_up_all = jnp.stack([ff_one_grads[0], ff_two_grads[0]])
        grad_down_all = jnp.stack([ff_one_grads[1], ff_two_grads[1]])
        grad_gain_all = jnp.concatenate(
            [cross_grads[2], jnp.stack([ff_one_grads[4], self_grads[2], ff_two_grads[4]])]
        )
        grad_shift_all = jnp.concatenate(
            [cross_grads[3], jnp.stack([ff_one_grads[5], self_grads[3], ff_two_grads[5]])]
        )
        grad_upb_all = jnp.stack([ff_one_grads[2], ff_two_grads[2]])
        grad_downb_all = jnp.stack([ff_one_grads[3], ff_two_grads[3]])
        grad_step = (
            grad_qkv_all,
            grad_out_all,
            grad_up_all,
            grad_down_all,
            grad_gain_all,
            grad_shift_all,
            grad_upb_all,
            grad_downb_all,
        )
        grad_sum = grad_step if grad_sum is None else jax.tree.map(jnp.add, grad_sum, grad_step)
    grad_sum = (
        lax.psum_scatter(grad_sum[0], "fsdp", scatter_dimension=2, tiled=True),
        lax.psum_scatter(grad_sum[1], "fsdp", scatter_dimension=1, tiled=True),
        lax.psum_scatter(grad_sum[2], "fsdp", scatter_dimension=1, tiled=True),
        lax.psum_scatter(grad_sum[3], "fsdp", scatter_dimension=1, tiled=True),
        lax.psum_scatter(grad_sum[4], "fsdp", scatter_dimension=1, tiled=True),
        lax.psum_scatter(grad_sum[5], "fsdp", scatter_dimension=1, tiled=True),
        lax.psum_scatter(grad_sum[6], "fsdp", scatter_dimension=1, tiled=True),
        lax.psum_scatter(grad_sum[7], "fsdp", scatter_dimension=1, tiled=True),
    )
    kv_part, gain_part, shift_part = (
        lax.psum(grad_sum[0][0, 1:3].astype(jnp.bfloat16), "seq").astype(jnp.float32),
        lax.psum(grad_sum[4][1].astype(jnp.bfloat16), "seq").astype(jnp.float32),
        lax.psum(grad_sum[5][1].astype(jnp.bfloat16), "seq").astype(jnp.float32),
    )
    qkv_final = grad_sum[0].at[0, 1:3].set(kv_part)
    gain_final = grad_sum[4].at[1].set(gain_part)
    shift_final = grad_sum[5].at[1].set(shift_part)
    return (
        jnp.stack(finals),
        jnp.stack(latent_grads),
        jnp.stack(token_grads),
        qkv_final,
        grad_sum[1],
        grad_sum[2],
        grad_sum[3],
        gain_final,
        shift_final,
        grad_sum[6],
        grad_sum[7],
    )


def solution(mesh):
    in_specs = (
        P(None, "fsdp", None, None),
        P(None, "fsdp", "seq", None),
        P(None, "fsdp"),
        P(None, "fsdp", None),
        P(None, None, "fsdp", None),
        P(None, "fsdp", None),
        P(None, "fsdp", None),
        P(None, "fsdp", None),
        P(None, "fsdp"),
        P(None, "fsdp"),
        P(None, "fsdp"),
        P(None, "fsdp"),
        P(None, "fsdp", None, None),
    )
    out_specs = (
        P(None, "fsdp", None, None),
        P(None, "fsdp", None, None),
        P(None, "fsdp", "seq", None),
        P(None, None, "fsdp", None),
        P(None, "fsdp", None),
        P(None, "fsdp", None),
        P(None, "fsdp", None),
        P(None, "fsdp"),
        P(None, "fsdp"),
        P(None, "fsdp"),
        P(None, "fsdp"),
    )
    return jax.shard_map(
        per_device, mesh=mesh, in_specs=in_specs, out_specs=out_specs, check_vma=False
    )
```

profile of v0, /device:TPU:0, one launch (start us, length us, event | category | flops | bytes accessed | tf_op | source)
XLA Modules:
  0.0 1272.3 jit_solution(13977146467657318002)
XLA Ops:
  8.0 10.5 all-gather.1
  18.5 8.8 all-gather
  32.8 10.1 fusion.290
  46.0 15.5 %all-gather.8.cloned.1.call-done = bf16[2,3,768,768]{3,2,1,0:T(8,128)(2,1)} async-done(((bf16[2,3,96,768]{3,2,1,0:T(8,128)(2,1)}), bf16[2,3,768,768]{3,2,1,0:T(8,128)(2,1)}) %all-gather.8.cloned.1.call-update) | async-done | bytes 7077904 | tf_op jit(solution)/shard_map/all_gather | solution.py:214
  130.3 8.7 all-gather.2
  140.4 8.0 all_gather.67
  149.6 18.7 %all-reduce.3 = (f32[1,128,12]{1,0,2:T(1,128)S(1)}, f32[1,128,12]{1,0,2:T(1,128)S(1)}) all-reduce(f32[1,128,12]{1,0,2:T(1,128)S(1)} %reduce_sum.702, f32[1,128,12]{1,0,2:T(1,128)S(1)} %reduce_sum.680), channel_id=5, replica_groups=mesh['fsdp'=8,'seq'=4] {'seq'}, use_global_device_ids=true, to_apply=%region_21.22.clone | all-reduce | flops 3072 | bytes 24576
  168.2 11.8 all_gather.71
  180.1 11.9 all_gather.64
  192.0 15.4 %all_gather.70 = f32[1,128,12,64]{1,3,0,2:T(8,128)S(1)} all-gather(f32[1,128,3,64]{1,3,0,2:T(8,128)} %bitcast.876), channel_id=1, replica_groups=mesh['fsdp'=8,'seq'=4] {'seq'}, dimensions={2}, use_global_device_ids=true | all-gather | bytes 491520 | tf_op jit(solution)/shard_map/all_gather | solution.py:119
  210.2 14.8 %all_gather.31 = f32[1,128,12,64]{1,3,0,2:T(8,128)S(1)} all-gather(f32[1,128,3,64]{1,3,0,2:T(8,128)} %bitcast.877), channel_id=1, replica_groups=mesh['fsdp'=8,'seq'=4] {'seq'}, dimensions={2}, use_global_device_ids=true | all-gather | bytes 491520 | tf_op jit(solution)/shard_map/all_gather | solution.py:119
  233.5 52.4 %all-gather.14.cloned.1.call-done = bf16[2,3072,768]{2,1,0:T(8,128)(2,1)} async-done(((bf16[2,384,768]{2,1,0:T(8,128)(2,1)}), bf16[2,3072,768]{2,1,0:T(8,128)(2,1)}) %all-gather.14.cloned.1.call-update) | async-done | bytes 9437200 | tf_op jit(solution)/shard_map/all_gather | solution.py:217
  392.7 7.5 convolution_convert_fusion
  423.8 7.5 convolution_convert_fusion.1
  464.1 10.5 fusion.75
  490.4 14.1 %all_gather.73 = bf16[1,128,12,64]{1,3,0,2:T(8,128)(2,1)S(1)} all-gather(bf16[1,128,3,64]{1,3,0,2:T(8,128)(2,1)} %bitcast.889), channel_id=1, replica_groups=mesh['fsdp'=8,'seq'=4] {'seq'}, dimensions={2}, use_global_device_ids=true | all-gather | bytes 245760 | tf_op jit(solution)/shard_map/all_gather | solution.py:163
  504.5 14.1 %all_gather.72 = bf16[1,128,12,64]{1,3,0,2:T(8,128)(2,1)S(1)} all-gather(bf16[1,128,3,64]{1,3,0,2:T(8,128)(2,1)} %bitcast.890), channel_id=1, replica_groups=mesh['fsdp'=8,'seq'=4] {'seq'}, dimensions={2}, use_global_device_ids=true | all-gather | bytes 245760 | tf_op jit(solution)/shard_map/all_gather | solution.py:163
  531.6 9.0 maximum_add_fusion.2
  540.6 21.6 %copy.326 = f32[2,3,768,768]{3,0,1,2:T(2,128)} copy(f32[2,3,768,768]{2,3,1,0:T(8,128)} %maximum_add_fusion.2) | data formatting | bytes 28311552 | tf_op jit(solution)/shard_map/add | solution.py:302
  592.6 11.7 bitcast_reduce_fusion.3
  604.7 9.0 fusion.17
  634.1 117.9 %all-reduce.10.cloned.1.call-done = f32[2,3,768,768]{3,0,1,2:T(2,128)} async-done(((f32[2,3,768,768]{3,0,1,2:T(2,128)}), f32[2,3,768,768]{3,0,1,2:T(2,128)}) %all-reduce.10.cloned.1.call-update) | async-done | bytes 14155792
  773.7 11.3 maximum_add_fusion
  797.6 11.8 maximum_add_fusion.1
  810.0 8.2 add_bitcast_fusion.1
  821.3 53.8 %copy.327 = f32[2,1,1578,768]{3,1,2,0:T(1,128)} copy(f32[2,1,1578,768]{3,2,1,0:T(8,128)S(1)} %pad_maximum_fusion) | data formatting | bytes 19390464
  886.8 18.8 %reduce-scatter.36.cloned.1.call-done = f32[96,5]{1,0:T(8,128)} async-done(((f32[768,5]{1,0:T(8,128)}), f32[96,5]{1,0:T(8,128)}) %reduce-scatter.36.cloned.1.call-update) | async-done | bytes 1936
  906.5 11.7 all-reduce.4
  920.4 26.9 %all-reduce.8.cloned.1.call-done = bf16[1,2,96,768]{3,0,1,2:T(2,128)(2,1)} async-done(((bf16[1,2,96,768]{3,0,1,2:T(2,128)(2,1)}), bf16[1,2,96,768]{3,0,1,2:T(2,128)(2,1)}) %all-reduce.8.cloned.1.call-update) | async-done | bytes 294928 | tf_op jit(solution)/shard_map/psum | solution.py:314
  956.2 49.0 %reduce-scatter.28.cloned.1.call-done = f32[2,96,768]{2,1,0:T(8,128)} async-done(((f32[2,768,768]{2,1,0:T(8,128)}), f32[2,96,768]{2,1,0:T(8,128)}) %reduce-scatter.28.cloned.1.call-update) | async-done | bytes 589840 | tf_op jit(solution)/shard_map/reduce_scatter | solution.py:305
  1005.2 130.2 %reduce-scatter.30.cloned.1.call-done = f32[2,96,3072]{2,1,0:T(8,128)} async-done(((f32[2,768,3072]{2,1,0:T(8,128)}), f32[2,96,3072]{2,1,0:T(8,128)}) %reduce-scatter.30.cloned.1.call-update) | async-done | bytes 2359312 | tf_op jit(solution)/shard_map/reduce_scatter | solution.py:306
  1135.4 130.2 %reduce-scatter.32.cloned.1.call-done = f32[2,384,768]{2,1,0:T(8,128)} async-done(((f32[2,3072,768]{2,1,0:T(8,128)}), f32[2,384,768]{2,1,0:T(8,128)}) %reduce-scatter.32.cloned.1.call-update) | async-done | bytes 2359312 | tf_op jit(solution)/shard_map/reduce_scatter | solution.py:307
  (823 shorter events, 390.5 us)
Async XLA Ops:
  7.2 54.4 %all-gather.8.cloned.1.call-start = ((), (), s32[]{:S(2)}) async-start(), calls=%async_computation.11 | async-start | bytes 7962624 | tf_op jit(solution)/shard_map/all_gather | solution.py:214
  7.9 184.1 %reduce-scatter.22.cloned.1.call-start = ((), (), s32[]{:S(2)}) async-start(), calls=%async_computation.16 | async-start | bytes 491520 | tf_op jit(solution)/shard_map/reduce_scatter | solution.py:115
  30.2 56.1 %copy-start.157 = (pred[1578]{0:T(1024)(128)(4,1)}, pred[1578]{0:T(1024)(128)(4,1)S(1)}, u32[]{:S(2)}) copy-start(pred[1578]{0:T(1024)(128)(4,1)S(1)} %fusion.235) | copy-start | bytes 4738
  30.3 67.2 %copy-start.186 = (f32[768]{0:T(1024)}, f32[768]{0:T(1024)S(1)}, u32[]{:S(2)}) copy-start(f32[768]{0:T(1024)S(1)} %get-tuple-element.153) | copy-start | bytes 9220
  30.3 267.9 %copy-start.123 = (f32[768]{0:T(1024)}, f32[768]{0:T(1024)S(1)}, u32[]{:S(2)}) copy-start(f32[768]{0:T(1024)S(1)} %get-tuple-element.151) | copy-start | bytes 9220
  30.3 289.6 %copy-start.125 = (f32[768]{0:T(1024)}, f32[768]{0:T(1024)S(1)}, u32[]{:S(2)}) copy-start(f32[768]{0:T(1024)S(1)} %get-tuple-element.149) | copy-start | bytes 9220
  30.3 306.5 %copy-start.121 = (f32[768]{0:T(1024)}, f32[768]{0:T(1024)S(1)}, u32[]{:S(2)}) copy-start(f32[768]{0:T(1024)S(1)} %get-tuple-element.270) | copy-start | bytes 9220
  32.8 62.1 %copy-start.215 = (f32[128]{0:T(128)}, f32[128]{0:T(128)S(1)}, u32[]{:S(2)}) copy-start(f32[128]{0:T(128)S(1)} %get-tuple-element.140) | copy-start | bytes 1540
  92.8 115.4 %all-gather.10.cloned.1.call-start = ((), (), s32[]{:S(2)}) async-start(), calls=%async_computation.13 | async-start | bytes 2654208 | tf_op jit(solution)/shard_map/all_gather | solution.py:215
  93.5 116.7 %reduce-scatter.20.cloned.1.call-start = ((), (), s32[]{:S(2)}) async-start(), calls=%async_computation.12 | async-start | bytes 491520 | tf_op jit(solution)/shard_map/reduce_scatter | solution.py:115
  129.1 100.0 %all-gather.12.cloned.1.call-start = ((), (), s32[]{:S(2)}) async-start(), calls=%async_computation.14 | async-start | bytes 10616832 | tf_op jit(solution)/shard_map/all_gather | solution.py:216
  129.7 156.2 %all-gather.14.cloned.1.call-start = ((), (), s32[]{:S(2)}) async-start(), calls=%async_computation.15 | async-start | bytes 10616832 | tf_op jit(solution)/shard_map/all_gather | solution.py:217
  130.3 360.1 %reduce-scatter.26.cloned.1.call-start = ((), (), s32[]{:S(2)}) async-start(), calls=%async_computation.18 | async-start | bytes 245760 | tf_op jit(solution)/shard_map/reduce_scatter | solution.py:160
  149.6 79.5 %copy-start.146 = (f32[1,3072]{1,0:T(1,128)}, f32[1,3072]{1,0:T(1,128)S(1)}, u32[]{:S(2)}) copy-start(f32[1,3072]{1,0:T(1,128)S(1)} %get-tuple-element.199) | copy-start | bytes 36868
  210.0 75.9 %copy-start.19 = (f32[128,768]{1,0:T(8,128)}, f32[128,768]{1,0:T(8,128)S(1)}, u32[]{:S(2)}) copy-start(f32[128,768]{1,0:T(8,128)S(1)} %get-tuple-element.232) | copy-start | bytes 1179652
  227.6 70.6 %copy-start.150 = (f32[128]{0:T(128)}, f32[128]{0:T(128)S(1)}, u32[]{:S(2)}) copy-start(f32[128]{0:T(128)S(1)} %broadcast_multiply_fusion.8) | copy-start | bytes 1540
  229.1 56.8 %copy-start.188 = (f32[768]{0:T(1024)S(1)}, f32[768]{0:T(1024)}, u32[]{:S(2)}) copy-start(f32[768]{0:T(1024)} %get-tuple-element.155) | copy-start | bytes 9220
  416.0 88.4 %reduce-scatter.24.cloned.1.call-start = ((), (), s32[]{:S(2)}) async-start(), calls=%async_computation.17 | async-start | bytes 245760 | tf_op jit(solution)/shard_map/reduce_scatter | solution.py:160
  463.6 288.4 %all-reduce.10.cloned.1.call-start = ((), (), s32[]{:S(2)}) async-start(), calls=%async_computation.27 | async-start | bytes 28311552
  562.3 319.3 %reduce-scatter.40.cloned.1.call-start = ((), (), s32[]{:S(2)}) async-start(), calls=%async_computation.26 | async-start | bytes 442368
  604.4 278.6 %reduce-scatter.38.cloned.1.call-start = ((), (), s32[]{:S(2)}) async-start(), calls=%async_computation.25 | async-start | bytes 1769472
  617.7 268.3 %reduce-scatter.34.cloned.1.call-start = ((), (), s32[]{:S(2)}) async-start(), calls=%async_computation.23 | async-start | bytes 442368
  624.6 130.0 %copy-start.109 = (bf16[12,64,128]{2,1,0:T(8,128)(2,1)S(1)}, bf16[12,64,128]{2,1,0:T(8,128)(2,1)}, u32[]{:S(2)}) copy-start(bf16[12,64,128]{2,1,0:T(8,128)(2,1)} %copy-done.108) | copy-start | bytes 589828
  624.6 130.0 %copy-start.115 = (bf16[128,768]{1,0:T(8,128)(2,1)S(1)}, bf16[128,768]{1,0:T(8,128)(2,1)}, u32[]{:S(2)}) copy-start(bf16[128,768]{1,0:T(8,128)(2,1)} %copy-done.114) | copy-start | bytes 589828
  624.6 281.0 %reduce-scatter.36.cloned.1.call-start = ((), (), s32[]{:S(2)}) async-start(), calls=%async_computation.24 | async-start | bytes 442368
  634.1 313.2 %all-reduce.8.cloned.1.call-start = ((), (), s32[]{:S(2)}) async-start(), calls=%async_computation.19 | async-start | bytes 1179648 | tf_op jit(solution)/shard_map/psum | solution.py:314
  754.5 250.6 %reduce-scatter.28.cloned.1.call-start = ((), (), s32[]{:S(2)}) async-start(), calls=%async_computation.20 | async-start | bytes 5308416 | tf_op jit(solution)/shard_map/reduce_scatter | solution.py:305
  761.5 373.9 %reduce-scatter.30.cloned.1.call-start = ((), (), s32[]{:S(2)}) async-start(), calls=%async_computation.21 | async-start | bytes 21233664 | tf_op jit(solution)/shard_map/reduce_scatter | solution.py:306
  785.0 480.6 %reduce-scatter.32.cloned.1.call-start = ((), (), s32[]{:S(2)}) async-start(), calls=%async_computation.22 | async-start | bytes 21233664 | tf_op jit(solution)/shard_map/reduce_scatter | solution.py:307
  821.2 53.8 %copy-start.15 = (f32[128,768]{1,0:T(8,128)S(1)}, f32[128,768]{1,0:T(8,128)}, u32[]{:S(2)}) copy-start(f32[128,768]{1,0:T(8,128)} %copy-done.13) | copy-start | bytes 1179652
  821.3 57.4 %slice-start.12 = ((s8[9437184]{0:T(1024)(128)(4,1)}), s8[1048576]{0:T(1024)(128)(4,1)S(1)}, s32[]{:S(2)}) async-start(s8[9437184]{0:T(1024)(128)(4,1)} %bitcast.909), calls=%async_computation.40 | async-start | bytes 2097152
  821.3 57.4 %slice-start.13 = ((s8[9437184]{0:T(1024)(128)(4,1)}), s8[4194304]{0:T(1024)(128)(4,1)S(1)}, s32[]{:S(2)}) async-start(s8[9437184]{0:T(1024)(128)(4,1)} %bitcast.909), calls=%async_computation.41 | async-start | bytes 8388608
  (238 other events, 1616.6 us)
Sparse Core Ops, SparseCore 0:
  9.9 51.5 all-gather.7
  92.9 20.5 reduce-scatter.21
  115.6 27.2 all-gather.9
  145.7 20.6 reduce-scatter.19
  168.2 56.9 all-gather.11
  227.0 58.8 all-gather.13
  416.2 19.3 reduce-scatter.25
  463.7 19.4 reduce-scatter.23
  562.4 189.5 all-reduce.9
  755.2 33.9 reduce-scatter.39
  792.9 38.4 reduce-scatter.37
  834.6 33.7 reduce-scatter.33
  871.7 33.8 reduce-scatter.35
  908.0 39.3 all-reduce.7
  951.6 53.5 reduce-scatter.27
  1009.2 126.1 reduce-scatter.29
  1139.4 126.1 reduce-scatter.31
where the time goes:
time: 1280 us; the launch traced here: 1270 us
  waiting for transfers between devices  544 us (42%)
  matrix products  246 us (19%)
  local copies, waits for them, and re-layouts  220 us (17%)
  blocking collectives  148 us (12%)
  other arithmetic  91.5 us (7%)
  between operations  20.5 us (2%)
    dot_general x78, matrix products, product(): return jnp.einsum(form, left, right, preferred_element_type=jnp.float32)  246 us
    unnamed x22, waiting for transfers between devices  139 us
    reduce_scatter x1, waiting for transfers between devices, per_device(): lax.psum_scatter(grad_sum[2], 'fsdp', scatter_dimension=1, tiled=True)  130 us
    reduce_scatter x1, waiting for transfers between devices, per_device(): lax.psum_scatter(grad_sum[3], 'fsdp', scatter_dimension=1, tiled=True)  130 us
    unnamed x525, local copies, waits for them, and re-layouts  90.3 us
    all_gather x1, waiting for transfers between devices, per_device(): lax.all_gather(mlp_out, 'fsdp', axis=1, tiled=True)  52.4 us
    reduce_scatter x1, waiting for transfers between devices, per_device(): lax.psum_scatter(grad_sum[1], 'fsdp', scatter_dimension=1, tiled=True)  49 us
    add x8, other arithmetic, per_device(): jax.tree.map(jnp.add, grad_sum, grad_step)  37.3 us
  transfers between devices with their start and end apart: 17, of which 8 were waited for; matrix products, arithmetic and copies ran while one was open for 27% of the time, Pallas kernels for 0%

commit v1 on v0

--- a/solution.py
+++ b/solution.py
@@ -9,6 +9,19 @@
 PATCHES = 392
 FRAMES = 16
 epsilon = 1e-06
+
+
+def ring_gather(x, axis, dim):
+    ways = lax.axis_size(axis)
+    up = [(d, (d + 1) % ways) for d in range(ways)]
+    down = [(d, (d - 1) % ways) for d in range(ways)]
+    earlier, later = ([x], [x])
+    for _ in range(ways // 2):
+        earlier.append(lax.ppermute(earlier[-1], axis, up))
+    for _ in range((ways - 1) // 2):
+        later.append(lax.ppermute(later[-1], axis, down))
+    line = jnp.concatenate([*earlier[::-1], *later[1:]], axis=dim)
+    return jnp.roll(line, (lax.axis_index(axis) - ways // 2) * x.shape[dim], axis=dim)
 
 
 def layer_norm(values, scales, offsets):
@@ -214,7 +227,7 @@
             lax.all_gather(qkv_weight, "fsdp", axis=2, tiled=True),
             lax.all_gather(out_weight, "fsdp", axis=1, tiled=True),
             lax.all_gather(mlp_in, "fsdp", axis=1, tiled=True),
-            lax.all_gather(mlp_out, "fsdp", axis=1, tiled=True),
+            ring_gather(mlp_out, "fsdp", 1),
             lax.all_gather(norm_gain, "fsdp", axis=1, tiled=True),
             lax.all_gather(norm_bias, "fsdp", axis=1, tiled=True),
             lax.all_gather(bias_in, "fsdp", axis=1, tiled=True),

time: 1280 us -> 1380 us (1.078)
  waiting for transfers between devices: 544 us -> 587 us
  other arithmetic: 91.5 us -> 113 us
  blocking collectives: 148 us -> 166 us
  starting transfers between devices: 2.18 us -> 18.9 us
    ppermute x0 -> x7, waiting for transfers between devices: none -> 105 us  [the longest x4 90.9 us: ring_gather(): earlier.append(lax.ppermute(earlier[-1], axis, up))]
    all_gather x1, waiting for transfers between devices: 52.4 us -> 0.01 us  [per_device(): lax.all_gather(mlp_out, 'fsdp', axis=1, tiled=True)]
    all_gather x1, blocking collectives: 8.7 us -> 26.4 us  [per_device(): lax.all_gather(bias_out, 'fsdp', axis=1, tiled=True)]
    unnamed x525 -> x626, local copies, waits for them, and re-layouts: 90.3 us -> 96 us
  transfers between devices with their start and end apart: 17 -> 24, of which waited for: 8 -> 12; matrix products, arithmetic and copies ran while one was open for 27% -> 29% of each run, Pallas kernels for 0% -> 0%
where the time goes in v1:
time: 1380 us; the launch traced here: 1370 us
  waiting for transfers between devices  587 us (43%)
  matrix products  241 us (17%)
  local copies, waits for them, and re-layouts  225 us (16%)
  blocking collectives  166 us (12%)
  other arithmetic  113 us (8%)
  between operations  21.1 us (2%)
  starting transfers between devices  18.9 us (1%)
    dot_general x78, matrix products, product(): return jnp.einsum(form, left, right, preferred_element_type=jnp.float32)  241 us
    unnamed x22, waiting for transfers between devices  130 us
    reduce_scatter x1, waiting for transfers between devices, per_device(): lax.psum_scatter(grad_sum[2], 'fsdp', scatter_dimension=1, tiled=True)  130 us
    reduce_scatter x1, waiting for transfers between devices, per_device(): lax.psum_scatter(grad_sum[3], 'fsdp', scatter_dimension=1, tiled=True)  130 us
    unnamed x626, local copies, waits for them, and re-layouts  96 us
    ppermute x4, waiting for transfers between devices, ring_gather(): earlier.append(lax.ppermute(earlier[-1], axis, up))  90.9 us
    reduce_scatter x1, waiting for transfers between devices, per_device(): lax.psum_scatter(grad_sum[1], 'fsdp', scatter_dimension=1, tiled=True)  49.1 us
    add x8, other arithmetic, per_device(): jax.tree.map(jnp.add, grad_sum, grad_step)  39.7 us
  transfers between devices with their start and end apart: 24, of which 12 were waited for; matrix products, arithmetic and copies ran while one was open for 29% of the time, Pallas kernels for 0%

profile of v1, /device:TPU:0, one launch (start us, length us, event | category | flops | bytes accessed | tf_op | source)
XLA Modules:
  0.0 1372.6 jit_solution(9944563871698447671)
XLA Ops:
  8.0 10.5 all-gather.1
  32.9 10.2 fusion.291
  46.2 15.4 %all-gather.8.cloned.1.call-done = bf16[2,3,768,768]{3,2,1,0:T(8,128)(2,1)} async-done(((bf16[2,3,96,768]{3,2,1,0:T(8,128)(2,1)}), bf16[2,3,768,768]{3,2,1,0:T(8,128)(2,1)}) %all-gather.8.cloned.1.call-update) | async-done | bytes 7077904 | tf_op jit(solution)/shard_map/all_gather | solution.py:227
  91.5 10.3 reduce-scatter.20.cloned.1.call-start
  134.1 18.9 %collective-permute-done = bf16[2,384,768]{2,1,0:T(8,128)(2,1)} collective-permute-done((bf16[2,384,768]{2,1,0:T(8,128)(2,1)S(1)}, bf16[2,384,768]{2,1,0:T(8,128)(2,1)}, u32[]{:S(2)}, u32[]{:S(2)}) %collective-permute-start) | collective-permute-done | bytes 1179680 | tf_op jit(solution)/shard_map/ppermute | solution.py:20
  155.6 31.3 %collective-permute-done.1 = bf16[2,384,768]{2,1,0:T(8,128)(2,1)S(1)} collective-permute-done((bf16[2,384,768]{2,1,0:T(8,128)(2,1)}, bf16[2,384,768]{2,1,0:T(8,128)(2,1)S(1)}, u32[]{:S(2)}, u32[]{:S(2)}) %collective-permute-start.1) | collective-permute-done | bytes 1179680 | tf_op jit(solution)/shard_map/ppermute | solution.py:20
  191.5 40.7 %collective-permute-done.2 = bf16[2,384,768]{2,1,0:T(8,128)(2,1)} collective-permute-done((bf16[2,384,768]{2,1,0:T(8,128)(2,1)S(1)}, bf16[2,384,768]{2,1,0:T(8,128)(2,1)}, u32[]{:S(2)}, u32[]{:S(2)}) %collective-permute-start.2) | collective-permute-done | bytes 1179680 | tf_op jit(solution)/shard_map/ppermute | solution.py:20
  232.2 26.4 %all-gather.2 = bf16[8,96,2]{1,2,0:T(2,128)(2,1)S(1)} all-gather(bf16[1,96,2]{1,2,0:T(2,128)(2,1)S(1)} %bitcast.912), channel_id=1, replica_groups=mesh['fsdp'=8,'seq'=4] {'fsdp'}, dimensions={0}, use_global_device_ids=true | all-gather | bytes 3456 | tf_op jit(solution)/shard_map/all_gather | solution.py:234
  276.4 12.1 collective-permute-done.6
  289.9 12.0 fusion.4
  301.8 18.9 %all-reduce.3 = (f32[1,128,12]{1,0,2:T(1,128)S(1)}, f32[1,128,12]{1,0,2:T(1,128)S(1)}) all-reduce(f32[1,128,12]{1,0,2:T(1,128)S(1)} %reduce_sum.702, f32[1,128,12]{1,0,2:T(1,128)S(1)} %reduce_sum.680), channel_id=5, replica_groups=mesh['fsdp'=8,'seq'=4] {'seq'}, use_global_device_ids=true, to_apply=%region_21.23.clone | all-reduce | flops 3072 | bytes 24576
  320.8 11.8 all_gather.68
  333.2 11.9 all_gather.62
  345.1 15.4 %all_gather.67 = f32[1,128,12,64]{1,3,0,2:T(8,128)S(1)} all-gather(f32[1,128,3,64]{1,3,0,2:T(8,128)} %bitcast.884), channel_id=1, replica_groups=mesh['fsdp'=8,'seq'=4] {'seq'}, dimensions={2}, use_global_device_ids=true | all-gather | bytes 491520 | tf_op jit(solution)/shard_map/all_gather | solution.py:132
  363.4 15.0 %all_gather.61 = f32[1,128,12,64]{1,3,0,2:T(8,128)S(1)} all-gather(f32[1,128,3,64]{1,3,0,2:T(8,128)} %bitcast.885), channel_id=1, replica_groups=mesh['fsdp'=8,'seq'=4] {'seq'}, dimensions={2}, use_global_device_ids=true | all-gather | bytes 491520 | tf_op jit(solution)/shard_map/all_gather | solution.py:132
  564.8 10.4 fusion.76
  591.1 13.9 %all_gather.71 = bf16[1,128,12,64]{1,3,0,2:T(8,128)(2,1)S(1)} all-gather(bf16[1,128,3,64]{1,3,0,2:T(8,128)(2,1)} %bitcast.897), channel_id=1, replica_groups=mesh['fsdp'=8,'seq'=4] {'seq'}, dimensions={2}, use_global_device_ids=true | all-gather | bytes 245760 | tf_op jit(solution)/shard_map/all_gather | solution.py:176
  604.9 13.9 %all_gather.70 = bf16[1,128,12,64]{1,3,0,2:T(8,128)(2,1)S(1)} all-gather(bf16[1,128,3,64]{1,3,0,2:T(8,128)(2,1)} %bitcast.898), channel_id=1, replica_groups=mesh['fsdp'=8,'seq'=4] {'seq'}, dimensions={2}, use_global_device_ids=true | all-gather | bytes 245760 | tf_op jit(solution)/shard_map/all_gather | solution.py:176
  632.3 10.6 maximum_add_fusion.2
  642.9 21.7 %copy.326 = f32[2,3,768,768]{3,0,1,2:T(2,128)} copy(f32[2,3,768,768]{2,3,1,0:T(8,128)} %maximum_add_fusion.2) | data formatting | bytes 28311552 | tf_op jit(solution)/shard_map/add | solution.py:315
  694.6 11.6 bitcast_reduce_fusion.3
  740.4 112.0 %all-reduce.10.cloned.1.call-done = f32[2,3,768,768]{3,0,1,2:T(2,128)} async-done(((f32[2,3,768,768]{3,0,1,2:T(2,128)}), f32[2,3,768,768]{3,0,1,2:T(2,128)}) %all-reduce.10.cloned.1.call-update) | async-done | bytes 14155792
  873.6 11.4 maximum_add_fusion
  896.7 11.8 maximum_add_fusion.1
  909.2 10.5 add_bitcast_fusion.1
  924.2 53.8 %copy.327 = f32[2,1,1578,768]{3,1,2,0:T(1,128)} copy(f32[2,1,1578,768]{3,2,1,0:T(8,128)S(1)} %pad_maximum_fusion) | data formatting | bytes 19390464
  989.8 16.1 %reduce-scatter.36.cloned.1.call-done = f32[96,5]{1,0:T(8,128)} async-done(((f32[768,5]{1,0:T(8,128)}), f32[96,5]{1,0:T(8,128)}) %reduce-scatter.36.cloned.1.call-update) | async-done | bytes 1936
  1006.8 11.7 all-reduce.4
  1020.7 26.9 %all-reduce.8.cloned.1.call-done = bf16[1,2,96,768]{3,0,1,2:T(2,128)(2,1)} async-done(((bf16[1,2,96,768]{3,0,1,2:T(2,128)(2,1)}), bf16[1,2,96,768]{3,0,1,2:T(2,128)(2,1)}) %all-reduce.8.cloned.1.call-update) | async-done | bytes 294928 | tf_op jit(solution)/shard_map/psum | solution.py:327
  1056.4 49.1 %reduce-scatter.28.cloned.1.call-done = f32[2,96,768]{2,1,0:T(8,128)} async-done(((f32[2,768,768]{2,1,0:T(8,128)}), f32[2,96,768]{2,1,0:T(8,128)}) %reduce-scatter.28.cloned.1.call-update) | async-done | bytes 589840 | tf_op jit(solution)/shard_map/reduce_scatter | solution.py:318
  1105.5 130.2 %reduce-scatter.30.cloned.1.call-done = f32[2,96,3072]{2,1,0:T(8,128)} async-done(((f32[2,768,3072]{2,1,0:T(8,128)}), f32[2,96,3072]{2,1,0:T(8,128)}) %reduce-scatter.30.cloned.1.call-update) | async-done | bytes 2359312 | tf_op jit(solution)/shard_map/reduce_scatter | solution.py:319
  1235.7 130.2 %reduce-scatter.32.cloned.1.call-done = f32[2,384,768]{2,1,0:T(8,128)} async-done(((f32[2,3072,768]{2,1,0:T(8,128)}), f32[2,384,768]{2,1,0:T(8,128)}) %reduce-scatter.32.cloned.1.call-update) | async-done | bytes 2359312 | tf_op jit(solution)/shard_map/reduce_scatter | solution.py:320
  (941 shorter events, 445.2 us)
Async XLA Ops:
  7.2 54.4 %all-gather.8.cloned.1.call-start = ((), (), s32[]{:S(2)}) async-start(), calls=%async_computation.11 | async-start | bytes 7962624 | tf_op jit(solution)/shard_map/all_gather | solution.py:227
  7.9 337.2 %reduce-scatter.22.cloned.1.call-start = ((), (), s32[]{:S(2)}) async-start(), calls=%async_computation.15 | async-start | bytes 491520 | tf_op jit(solution)/shard_map/reduce_scatter | solution.py:128
  30.3 360.8 %copy-start.124 = (f32[768]{0:T(1024)}, f32[768]{0:T(1024)S(1)}, u32[]{:S(2)}) copy-start(f32[768]{0:T(1024)S(1)} %get-tuple-element.152) | copy-start | bytes 9220
  30.3 368.6 %copy-start.152 = (f32[768]{0:T(1024)}, f32[768]{0:T(1024)S(1)}, u32[]{:S(2)}) copy-start(f32[768]{0:T(1024)S(1)} %get-tuple-element.270) | copy-start | bytes 9220
  30.3 368.6 %copy-start.159 = (f32[768]{0:T(1024)}, f32[768]{0:T(1024)S(1)}, u32[]{:S(2)}) copy-start(f32[768]{0:T(1024)S(1)} %get-tuple-element.151) | copy-start | bytes 9220
  30.3 385.6 %copy-start.126 = (f32[768]{0:T(1024)}, f32[768]{0:T(1024)S(1)}, u32[]{:S(2)}) copy-start(f32[768]{0:T(1024)S(1)} %get-tuple-element.150) | copy-start | bytes 9220
  30.4 404.1 %copy-start.122 = (f32[768]{0:T(1024)}, f32[768]{0:T(1024)S(1)}, u32[]{:S(2)}) copy-start(f32[768]{0:T(1024)S(1)} %get-tuple-element.271) | copy-start | bytes 9220
  90.8 270.6 %all-gather.10.cloned.1.call-start = ((), (), s32[]{:S(2)}) async-start(), calls=%async_computation.13 | async-start | bytes 2654208 | tf_op jit(solution)/shard_map/all_gather | solution.py:228
  91.5 271.9 %reduce-scatter.20.cloned.1.call-start = ((), (), s32[]{:S(2)}) async-start(), calls=%async_computation.12 | async-start | bytes 491520 | tf_op jit(solution)/shard_map/reduce_scatter | solution.py:128
  130.0 128.6 %copy-start.254 = (bf16[2,384]{1,0:T(2,128)(2,1)S(1)}, bf16[2,384]{1,0:T(2,128)(2,1)}, u32[]{:S(2)}) copy-start(bf16[2,384]{1,0:T(2,128)(2,1)} %param.31) | copy-start | bytes 4612
  130.0 138.9 %copy-start.276 = (u32[32]{0:T(128)S(1)}, u32[32]{0:T(128)}, u32[]{:S(2)}) copy-start(u32[32]{0:T(128)} %constant.192) | copy-start | bytes 388
  132.8 248.5 %all-gather.12.cloned.1.call-start = ((), (), s32[]{:S(2)}) async-start(), calls=%async_computation.14 | async-start | bytes 10616832 | tf_op jit(solution)/shard_map/all_gather | solution.py:229
  133.4 284.6 %all-gather.14.cloned.1.call-start = ((), (), s32[]{:S(2)}) async-start(), calls=%async_computation.16 | async-start | bytes 10616832 | tf_op jit(solution)/shard_map/all_gather | solution.py:266
  133.5 19.4 %collective-permute-start = (bf16[2,384,768]{2,1,0:T(8,128)(2,1)S(1)}, bf16[2,384,768]{2,1,0:T(8,128)(2,1)}, u32[]{:S(2)}, u32[]{:S(2)}) collective-permute-start(bf16[2,384,768]{2,1,0:T(8,128)(2,1)S(1)} %copy-done.46), channel_id=1, source_target_pairs={{0,4},{4,8},{8,12},{12,16},{16,20},{20,24},{24,28},{28,0},{1,5},{5... | collective-permute-start | bytes 3538952 | tf_op jit(solution)/shard_map/ppermute | solution.py:20
  134.0 457.0 %reduce-scatter.26.cloned.1.call-start = ((), (), s32[]{:S(2)}) async-start(), calls=%async_computation.18 | async-start | bytes 245760 | tf_op jit(solution)/shard_map/reduce_scatter | solution.py:173
  152.9 34.0 %collective-permute-start.1 = (bf16[2,384,768]{2,1,0:T(8,128)(2,1)}, bf16[2,384,768]{2,1,0:T(8,128)(2,1)S(1)}, u32[]{:S(2)}, u32[]{:S(2)}) collective-permute-start(bf16[2,384,768]{2,1,0:T(8,128)(2,1)} %collective-permute-done), channel_id=1, source_target_pairs={{0,4},{4,8},{8,12},{12,16},{16,20},{20,24},{24,28},{28,0},{1,5},{5... | collective-permute-start | bytes 3538952 | tf_op jit(solution)/shard_map/ppermute | solution.py:20
  152.9 35.7 %collective-permute-start.4 = (bf16[2,384,768]{2,1,0:T(8,128)(2,1)S(1)}, bf16[2,384,768]{2,1,0:T(8,128)(2,1)S(1)}, u32[]{:S(2)}, u32[]{:S(2)}) collective-permute-start(bf16[2,384,768]{2,1,0:T(8,128)(2,1)S(1)} %copy-done.47), channel_id=1, source_target_pairs={{0,28},{4,0},{8,4},{12,8},{16,12},{20,16},{24,20},{28,24},{1,29},{... | collective-permute-start | bytes 3538952 | tf_op jit(solution)/shard_map/ppermute | solution.py:22
  186.9 45.3 %collective-permute-start.2 = (bf16[2,384,768]{2,1,0:T(8,128)(2,1)S(1)}, bf16[2,384,768]{2,1,0:T(8,128)(2,1)}, u32[]{:S(2)}, u32[]{:S(2)}) collective-permute-start(bf16[2,384,768]{2,1,0:T(8,128)(2,1)S(1)} %collective-permute-done.1), channel_id=1, source_target_pairs={{0,4},{4,8},{8,12},{12,16},{16,20},{20,24},{24,28},{28,0},{1,5},{5... | collective-permute-start | bytes 3538952 | tf_op jit(solution)/shard_map/ppermute | solution.py:20
  188.6 78.8 %collective-permute-start.5 = (bf16[2,384,768]{2,1,0:T(8,128)(2,1)S(1)}, bf16[2,384,768]{2,1,0:T(8,128)(2,1)}, u32[]{:S(2)}, u32[]{:S(2)}) collective-permute-start(bf16[2,384,768]{2,1,0:T(8,128)(2,1)S(1)} %collective-permute-done.4), channel_id=1, source_target_pairs={{0,28},{4,0},{8,4},{12,8},{16,12},{20,16},{24,20},{28,24},{1,29},{... | collective-permute-start | bytes 3538952 | tf_op jit(solution)/shard_map/ppermute | solution.py:22
  232.2 38.6 %collective-permute-start.3 = (bf16[2,384,768]{2,1,0:T(8,128)(2,1)}, bf16[2,384,768]{2,1,0:T(8,128)(2,1)}, u32[]{:S(2)}, u32[]{:S(2)}) collective-permute-start(bf16[2,384,768]{2,1,0:T(8,128)(2,1)} %collective-permute-done.2), channel_id=1, source_target_pairs={{0,4},{4,8},{8,12},{12,16},{16,20},{20,24},{24,28},{28,0},{1,5},{5... | collective-permute-start | bytes 3538952 | tf_op jit(solution)/shard_map/ppermute | solution.py:20
  267.4 21.1 %collective-permute-start.6 = (bf16[2,384,768]{2,1,0:T(8,128)(2,1)}, bf16[2,384,768]{2,1,0:T(8,128)(2,1)}, u32[]{:S(2)}, u32[]{:S(2)}) collective-permute-start(bf16[2,384,768]{2,1,0:T(8,128)(2,1)} %collective-permute-done.5), channel_id=1, source_target_pairs={{0,28},{4,0},{8,4},{12,8},{16,12},{20,16},{24,20},{28,24},{1,29},{... | collective-permute-start | bytes 3538952 | tf_op jit(solution)/shard_map/ppermute | solution.py:22
  516.7 88.2 %reduce-scatter.24.cloned.1.call-start = ((), (), s32[]{:S(2)}) async-start(), calls=%async_computation.17 | async-start | bytes 245760 | tf_op jit(solution)/shard_map/reduce_scatter | solution.py:173
  564.5 287.9 %all-reduce.10.cloned.1.call-start = ((), (), s32[]{:S(2)}) async-start(), calls=%async_computation.27 | async-start | bytes 28311552
  664.6 319.9 %reduce-scatter.40.cloned.1.call-start = ((), (), s32[]{:S(2)}) async-start(), calls=%async_computation.26 | async-start | bytes 442368
  706.2 279.7 %reduce-scatter.38.cloned.1.call-start = ((), (), s32[]{:S(2)}) async-start(), calls=%async_computation.25 | async-start | bytes 1769472
  722.8 266.2 %reduce-scatter.34.cloned.1.call-start = ((), (), s32[]{:S(2)}) async-start(), calls=%async_computation.23 | async-start | bytes 442368
  724.6 130.3 %copy-start.110 = (bf16[12,64,128]{2,1,0:T(8,128)(2,1)S(1)}, bf16[12,64,128]{2,1,0:T(8,128)(2,1)}, u32[]{:S(2)}) copy-start(bf16[12,64,128]{2,1,0:T(8,128)(2,1)} %copy-done.109) | copy-start | bytes 589828
  729.6 276.3 %reduce-scatter.36.cloned.1.call-start = ((), (), s32[]{:S(2)}) async-start(), calls=%async_computation.24 | async-start | bytes 442368
  740.3 307.3 %all-reduce.8.cloned.1.call-start = ((), (), s32[]{:S(2)}) async-start(), calls=%async_computation.19 | async-start | bytes 1179648 | tf_op jit(solution)/shard_map/psum | solution.py:327
  854.9 250.6 %reduce-scatter.28.cloned.1.call-start = ((), (), s32[]{:S(2)}) async-start(), calls=%async_computation.20 | async-start | bytes 5308416 | tf_op jit(solution)/shard_map/reduce_scatter | solution.py:318
  861.4 374.3 %reduce-scatter.30.cloned.1.call-start = ((), (), s32[]{:S(2)}) async-start(), calls=%async_computation.21 | async-start | bytes 21233664 | tf_op jit(solution)/shard_map/reduce_scatter | solution.py:319
  884.9 480.9 %reduce-scatter.32.cloned.1.call-start = ((), (), s32[]{:S(2)}) async-start(), calls=%async_computation.22 | async-start | bytes 21233664 | tf_op jit(solution)/shard_map/reduce_scatter | solution.py:320
  (292 other events, 3101.2 us)
Sparse Core Ops, SparseCore 0:
  9.9 51.5 all-gather.7
  90.9 20.5 reduce-scatter.21
  113.6 28.3 all-gather.9
  144.8 20.9 reduce-scatter.19
  167.5 82.7 all-gather.11
  252.1 73.9 all-gather.13
  516.8 17.4 reduce-scatter.25
  564.6 17.4 reduce-scatter.23
  664.7 187.5 all-reduce.9
  855.6 33.9 reduce-scatter.39
  893.2 38.4 reduce-scatter.37
  934.9 33.7 reduce-scatter.33
  972.1 33.8 reduce-scatter.35
  1008.2 39.3 all-reduce.7
  1051.9 53.5 reduce-scatter.27
  1109.5 126.1 reduce-scatter.29
  1239.7 126.1 reduce-scatter.31
